TPU v7x, 512 devices: a whole 4x8x8 slice. The times are simulated.
512 devices in a mesh: batch: 8 (over y), grp: 64 (over x, z, core).
Axes of the slice: x: 4, y: 8, z: 8, core: 2. Of those that a mesh axis runs over, the one named last changes fastest.
Arguments:
- amps: bfloat16 [24, 64, 1024, 128], P('batch', None, 'grp'), may hold values from -6 to 6
- cycle_inter: bfloat16 [24, 1024, 8, 128], P('batch', 'grp'), may hold values from -0.109375 to 0.109375
- k_irrep: int32 [24], replicated, may hold values from 0 to 7
- i_irrep: int32 [64], replicated, may hold values from 0 to 7
- j_irrep: int32 [8], replicated, may hold values from 0 to 7
- virt_count: int32 [8], replicated, may hold values from 64 to 128, as said below
Outputs:
- cycle_term: bfloat16 [64, 8, 1024, 128], P(None, 'batch', 'grp')
Inputs may be any that keep to these rules, and one draw needn't show every extreme that they name: `virt_count`: together the counts are 800.
All inputs are finite; a program needn't handle non-finite values.
Results may differ from a plain program's by a relative error of at most 0.013.
Values may be sent and summed in bfloat16 or wider, within the bound.
A program may use at most 64 MiB of HBM per device.

v0:
```python
import jax
import jax.numpy as jnp
from jax import lax
from jax.sharding import PartitionSpec as P


def shards(amps, cycle_inter, k_irrep, i_irrep, j_irrep, virt_count):
    k_local = amps.shape[0]
    slab_size = amps.shape[2]
    width = amps.shape[3]
    n_irrep = virt_count.shape[0]
    j_total = cycle_inter.shape[2]
    irreps = jnp.arange(n_irrep, dtype=jnp.int32)
    slot_pos = jnp.arange(width, dtype=jnp.int32)

    def count_of(labels):
        return jnp.sum(jnp.where(labels[..., None] == irreps, virt_count, 0), axis=-1)

    k_first = lax.axis_index("batch") * k_local
    k_labels = lax.dynamic_slice_in_dim(k_irrep, k_first, k_local)
    c_index = lax.axis_index("grp") * slab_size + jnp.arange(slab_size, dtype=jnp.int32)
    c_labels = c_index // width
    c_live = c_index % width < count_of(c_labels)
    a_labels = jnp.bitwise_xor(
        jnp.bitwise_xor(k_labels[:, None, None], i_irrep[None, :, None]), c_labels[None, None, :]
    )
    amp_mask = c_live[None, None, :, None] & (slot_pos < count_of(a_labels)[..., None])
    masked_amps = jnp.where(amp_mask, amps, jnp.zeros((), amps.dtype))
    b_labels = jnp.bitwise_xor(
        jnp.bitwise_xor(k_labels[:, None, None], c_labels[None, :, None]), j_irrep[None, None, :]
    )
    inter_mask = c_live[None, :, None, None] & (slot_pos < count_of(b_labels)[..., None])
    masked_inter = jnp.where(inter_mask, cycle_inter, jnp.zeros((), cycle_inter.dtype))
    sorted_amps = lax.all_to_all(masked_amps, "grp", split_axis=1, concat_axis=2, tiled=True)
    whole_inter = lax.all_gather(masked_inter, "grp", axis=1, tiled=True)
    i_count = sorted_amps.shape[1]
    i_labels = lax.dynamic_slice_in_dim(i_irrep, lax.axis_index("grp") * i_count, i_count)
    k_source = jnp.bitwise_xor(irreps[None, :], k_labels[:, None])
    amp_blocks = sorted_amps.reshape(k_local, i_count, n_irrep, width, width)
    amp_perm = jnp.take_along_axis(amp_blocks, k_source[:, None, :, None, None], axis=2)
    inter_blocks = whole_inter.reshape(k_local, n_irrep, width, j_total, width)
    inter_perm = jnp.take_along_axis(inter_blocks, k_source[:, :, None, None, None], axis=1)
    products = jnp.einsum(
        "kiqca,kqcjb->iqajb", amp_perm, inter_perm, preferred_element_type=jnp.float32
    )
    i_source = jnp.bitwise_xor(irreps[None, :], i_labels[:, None])
    partial_value = jnp.take_along_axis(products, i_source[:, :, None, None, None], axis=1)
    partial_value = jnp.transpose(partial_value, (0, 3, 1, 2, 4)).reshape(
        i_count, j_total, n_irrep * width, width
    )
    rounded = partial_value.astype(jnp.bfloat16)
    resorted = lax.all_to_all(rounded, "grp", split_axis=2, concat_axis=0, tiled=True)
    return lax.psum_scatter(
        resorted.astype(jnp.float32).astype(jnp.bfloat16), "batch", scatter_dimension=1, tiled=True
    )


def solution(mesh):
    return jax.shard_map(
        shards,
        mesh=mesh,
        in_specs=(P("batch", None, "grp", None), P("batch", "grp", None, None), P(), P(), P(), P()),
        out_specs=P(None, "batch", "grp", None),
        check_vma=False,
    )
```

profile of v0, /device:TPU:1, one launch (start us, length us, event | category | flops | bytes accessed | tf_op | source)
XLA Modules:
  0.0 229.7 jit_solution(9864530524184369395)
XLA Ops:
  6.6 0.7 dynamic_slice.7
  7.3 0.1 broadcast_xor_fusion.3
  7.4 0.7 select_reduce_fusion.2
  8.1 0.7 broadcast_xor_fusion.1
  8.8 0.8 select_reduce_fusion.1
  9.6 0.1 copy.26
  9.7 1.7 fusion.11
  11.4 0.7 broadcast_xor_fusion.2
  12.1 0.1 broadcast_xor_fusion
  12.2 0.8 select_reduce_fusion
  13.0 0.1 copy.27
  13.1 2.3 %fusion.8 = bf16[3,64,16,128]{3,2,0,1:T(8,128)(2,1)} fusion(bf16[3,64,16,128]{3,2,1,0:T(8,128)(2,1)} %param.6, s32[3,64,16]{2,0,1:T(4,128)S(1)} %copy.27, pred[16]{0:T(512)(128)(4,1)S(1)} %fusion.18), kind=kLoop, calls=%fused_computation.12 | loop fusion | flops 1179648 | bytes 1585168 | tf_op jit(solution)/shard_map/jit(_where)/select_n | solution.py:28
  15.4 14.8 %all-to-all-start = ((bf16[3,64,16,128]{3,2,0,1:T(8,128)(2,1)}), bf16[3,64,16,128]{3,2,0,1:T(8,128)(2,1)S(1)}, u32[]{:S(2)}, u32[]{:S(2)}) async-start(bf16[3,64,16,128]{3,2,0,1:T(8,128)(2,1)} %fusion.8), calls=%async_computation | async-start | bytes 1572864 | tf_op jit(solution)/shard_map/all_to_all | solution.py:34
  30.3 0.1 fusion.14
  30.4 0.1 reshape.379
  30.5 0.6 dynamic_slice.6
  31.1 0.6 fusion.19
  31.7 0.6 compare_and_fusion
  32.4 0.1 fusion.17
  32.5 23.5 %all-to-all-done = bf16[3,64,16,128]{3,2,0,1:T(8,128)(2,1)S(1)} async-done(((bf16[3,64,16,128]{3,2,0,1:T(8,128)(2,1)}), bf16[3,64,16,128]{3,2,0,1:T(8,128)(2,1)S(1)}, u32[]{:S(2)}, u32[]{:S(2)}) %all-to-all-start) | async-done | bytes 786464 | tf_op jit(solution)/shard_map/all_to_all | solution.py:34
  55.9 0.1 copy.29
  56.1 0.8 gather_fusion.2
  56.8 48.2 %all-gather.2.cloned.1.call-done = bf16[3,1024,8,128]{3,2,1,0:T(8,128)(2,1)} async-done(((bf16[3,16,8,128]{3,2,1,0:T(8,128)(2,1)}), bf16[3,1024,8,128]{3,2,1,0:T(8,128)(2,1)}) %all-gather.2.cloned.1.call-update) | async-done | bytes 6291472 | tf_op jit(solution)/shard_map/all_gather | solution.py:35
  105.0 7.4 %gather_fusion.1 = bf16[24,128,8,128]{3,2,1,0:T(8,128)(2,1)} fusion(bf16[3,8,128,8,128]{4,3,2,1,0:T(8,128)(2,1)} %bitcast.40, s32[24]{0:T(128)S(1)} %reshape.379), kind=kCustom, calls=%fused_computation.1 | custom fusion | bytes 12583104 | tf_op jit(solution)/shard_map/jit(take_along_axis)/gather | solution.py:42
  112.4 3.4 %broadcast_select_fusion = bf16[3,8,128,8,128]{4,3,2,1,0:T(8,128)(2,1)S(1)} fusion(bf16[3,8,128,8,128]{4,3,2,1,0:T(8,128)(2,1)} %bitcast.37, pred[3,8]{1,0:T(4,128)(4,1)S(1)} %fusion.17), kind=kLoop, calls=%fused_computation.5 | loop fusion | flops 3145728 | bytes 12582936 | tf_op jit(solution)/shard_map/jit(take_along_axis)/select_n | solution.py:42
  115.8 3.5 %fusion.3 = bf16[8,128,8,128]{1,3,2,0:T(8,128)(2,1)} fusion(bf16[3,8,128,8,128]{4,3,2,1,0:T(8,128)(2,1)S(1)} %broadcast_select_fusion, bf16[3,8,128,128]{3,2,1,0:T(8,128)(2,1)S(1)} %bitcast.42, pred[3,8]{1,0:T(4,128)(4,1)S(1)} %fusion.17), kind=kOutput, calls=%fused_computation.8 | convolution fusion | flops 805699584 | bytes 9175064 | tf_op jit(solution)/shard_map/kiqca,kqcjb->iqajb/dot_general | solution.py:43
  119.4 2.5 %gather_fusion = bf16[8,128,8,128]{1,3,2,0:T(8,128)(2,1)S(1)} fusion(bf16[8,128,8,128]{1,3,2,0:T(8,128)(2,1)} %fusion.3, s32[1024]{0:T(1024)S(1)} %pad_clamp_fusion), kind=kCustom, calls=%fused_computation | custom fusion | bytes 4194336 | tf_op jit(solution)/shard_map/jit(take_along_axis)/gather | solution.py:47
  121.9 2.0 fusion.6
  123.9 3.2 %copy.40 = bf16[1,8,8,128,128]{4,1,3,2,0:T(8,128)(2,1)S(1)} copy(bf16[1,8,8,128,128]{3,4,1,2,0:T(8,128)(2,1)} %fusion.6) | data formatting | bytes 4194304 | tf_op jit(solution)/shard_map/convert_element_type | solution.py:51
  127.1 56.9 %all_to_all.27 = bf16[1,8,1024,128]{3,1,0,2:T(8,128)(2,1)S(1)} all-to-all(bf16[1,8,1024,128]{3,1,0,2:T(8,128)(2,1)S(1)} %bitcast.39), channel_id=1, replica_groups=mesh['batch'=8,'grp'=64] {'grp'}, dimensions={2} | all-to-all | bytes 4194304 | tf_op jit(solution)/shard_map/all_to_all | solution.py:52
  184.1 1.7 copy.34
  185.8 37.1 %reduce-scatter.2.cloned.1.call-done = bf16[64,1,16,128]{3,2,0,1:T(8,128)(2,1)} async-done(((bf16[64,8,16,128]{3,2,0,1:T(8,128)(2,1)}), bf16[64,1,16,128]{3,2,0,1:T(8,128)(2,1)}) %reduce-scatter.2.cloned.1.call-update) | async-done | bytes 262160 | tf_op jit(solution)/shard_map/reduce_scatter | solution.py:53
  (9 shorter events, 0.1 us)
Async XLA Ops:
  6.5 23.9 %copy-start = (s32[64]{0:T(128)S(1)}, s32[64]{0:T(128)}, u32[]{:S(2)}) copy-start(s32[64]{0:T(128)} %param.9) | copy-start | bytes 772
  6.5 98.5 %all-gather.2.cloned.1.call-start = ((), (), s32[]{:S(2)}) async-start(), calls=%async_computation.3 | async-start | bytes 6389760 | tf_op jit(solution)/shard_map/all_gather | solution.py:35
  15.4 40.5 %all-to-all-start = ((bf16[3,64,16,128]{3,2,0,1:T(8,128)(2,1)}), bf16[3,64,16,128]{3,2,0,1:T(8,128)(2,1)S(1)}, u32[]{:S(2)}, u32[]{:S(2)}) async-start(bf16[3,64,16,128]{3,2,0,1:T(8,128)(2,1)} %fusion.8), calls=%async_computation | async-start | bytes 1572864 | tf_op jit(solution)/shard_map/all_to_all | solution.py:34
  30.2 192.6 %reduce-scatter.2.cloned.1.call-start = ((), (), s32[]{:S(2)}) async-start(), calls=%async_computation.4 | async-start | bytes 2359296 | tf_op jit(solution)/shard_map/reduce_scatter | solution.py:53
Sparse Core Ops, SparseCore 0:
  11.5 93.4 all-gather.1
  185.9 36.8 reduce-scatter.1
where the time goes:
time: 234 us; the launch traced here: 230 us
  waiting for transfers between devices  109 us (47%)
  blocking collectives  56.9 us (24%)
  local copies, waits for them, and re-layouts  17.3 us (7%)
  starting transfers between devices  14.9 us (6%)
  other arithmetic  14.8 us (6%)
  between operations  13.5 us (6%)
  matrix products  3.53 us (2%)
    all_to_all x1, blocking collectives, shards(): lax.all_to_all(rounded, 'grp', split_axis=2, concat_axis=0, tiled=True)  56.9 us
    all_gather x1, waiting for transfers between devices, shards(): whole_inter = lax.all_gather(masked_inter, 'grp', axis=1, tiled=True)  48.2 us
    reduce_scatter x1, waiting for transfers between devices, shards(): lax.psum_scatter(resorted.astype(jnp.float32).astype(jnp.bfloat16), 'batc...  37.1 us
    all_to_all x1, waiting for transfers between devices, shards(): lax.all_to_all(masked_amps, 'grp', split_axis=1, concat_axis=2, tiled=True)  23.5 us
    all_to_all x1, starting transfers between devices, shards(): lax.all_to_all(masked_amps, 'grp', split_axis=1, concat_axis=2, tiled=True)  14.8 us
    gather x2, local copies, waits for them, and re-layouts, shards(): jnp.take_along_axis(inter_blocks, k_source[:, :, None, None, None], axis=1)  7.46 us
  transfers between devices with their start and end apart: 3, of which 3 were waited for; matrix products, arithmetic and copies ran while one was open for 3% of the time, Pallas kernels for 0%

commit v1 on v0

--- a/solution.py
+++ b/solution.py
@@ -49,10 +49,10 @@
         i_count, j_total, n_irrep * width, width
     )
     rounded = partial_value.astype(jnp.bfloat16)
-    resorted = lax.all_to_all(rounded, "grp", split_axis=2, concat_axis=0, tiled=True)
-    return lax.psum_scatter(
-        resorted.astype(jnp.float32).astype(jnp.bfloat16), "batch", scatter_dimension=1, tiled=True
-    )
+    summed = lax.psum_scatter(rounded, "batch", scatter_dimension=1, tiled=True)
+    outgoing = summed.reshape(-1, slab_size, width)
+    arrived = lax.all_to_all(outgoing, "grp", split_axis=0, concat_axis=0, tiled=True)
+    return arrived.reshape(-1, 1, slab_size, width)
 
 
 def solution(mesh):

time: 234 us -> 200 us (0.85); the launches traced: 230 us -> 200 us
  blocking collectives: 56.9 us -> 27.2 us
    all_to_all x1, blocking collectives: 56.9 us -> 27.2 us  [shards(): lax.all_to_all(outgoing, 'grp', split_axis=0, concat_axis=0, tiled=True)]
  transfers between devices with their start and end apart: 3 -> 3, of which waited for: 3 -> 3; matrix products, arithmetic and copies ran while one was open for 3% -> 4% of each run, Pallas kernels for 0% -> 0%
where the time goes in v1:
time: 200 us
  waiting for transfers between devices  108 us (54%)
  blocking collectives  27.2 us (14%)
  local copies, waits for them, and re-layouts  17.7 us (9%)
  starting transfers between devices  14.9 us (7%)
  other arithmetic  14.8 us (7%)
  between operations  13.5 us (7%)
  matrix products  3.53 us (2%)
    all_gather x1, waiting for transfers between devices, shards(): whole_inter = lax.all_gather(masked_inter, 'grp', axis=1, tiled=True)  48.2 us
    reduce_scatter x1, waiting for transfers between devices, shards(): summed = lax.psum_scatter(rounded, 'batch', scatter_dimension=1, tiled=True)  37.3 us
    all_to_all x1, blocking collectives, shards(): lax.all_to_all(outgoing, 'grp', split_axis=0, concat_axis=0, tiled=True)  27.2 us
    all_to_all x1, waiting for transfers between devices, shards(): lax.all_to_all(masked_amps, 'grp', split_axis=1, concat_axis=2, tiled=True)  22.7 us
    all_to_all x1, starting transfers between devices, shards(): lax.all_to_all(masked_amps, 'grp', split_axis=1, concat_axis=2, tiled=True)  14.8 us
    gather x2, local copies, waits for them, and re-layouts, shards(): jnp.take_along_axis(inter_blocks, k_source[:, :, None, None, None], axis=1)  7.46 us
  transfers between devices with their start and end apart: 3, of which 3 were waited for; matrix products, arithmetic and copies ran while one was open for 4% of the time, Pallas kernels for 0%

profile of v1, /device:TPU:1, one launch (start us, length us, event | category | flops | bytes accessed | tf_op | source)
XLA Modules:
  0.0 199.8 jit_solution(11525802815132884186)
XLA Ops:
  6.5 0.7 dynamic_slice.7
  7.3 0.1 broadcast_xor_fusion.3
  7.4 0.7 select_reduce_fusion.2
  8.1 0.7 broadcast_xor_fusion.1
  8.8 0.8 select_reduce_fusion.1
  9.6 0.1 copy.19
  9.7 1.7 fusion.11
  11.4 0.7 broadcast_xor_fusion.2
  12.1 0.1 broadcast_xor_fusion
  12.2 0.8 select_reduce_fusion
  13.0 0.1 copy.20
  13.1 2.3 %fusion.8 = bf16[3,64,16,128]{3,2,0,1:T(8,128)(2,1)} fusion(bf16[3,64,16,128]{3,2,1,0:T(8,128)(2,1)} %param.6, s32[3,64,16]{2,0,1:T(4,128)S(1)} %copy.20, pred[16]{0:T(512)(128)(4,1)S(1)} %fusion.18), kind=kLoop, calls=%fused_computation.12 | loop fusion | flops 1179648 | bytes 1585168 | tf_op jit(solution)/shard_map/jit(_where)/select_n | solution.py:28
  15.4 14.8 %all-to-all-start = ((bf16[3,64,16,128]{3,2,0,1:T(8,128)(2,1)}), bf16[3,64,16,128]{3,2,0,1:T(8,128)(2,1)S(1)}, u32[]{:S(2)}, u32[]{:S(2)}) async-start(bf16[3,64,16,128]{3,2,0,1:T(8,128)(2,1)} %fusion.8), calls=%async_computation | async-start | bytes 1572864 | tf_op jit(solution)/shard_map/all_to_all | solution.py:34
  30.3 0.1 fusion.14
  30.4 0.1 reshape.387
  30.5 1.3 dynamic_slice.6
  31.7 0.6 fusion.19
  32.4 0.6 compare_and_fusion
  33.0 0.1 fusion.17
  33.1 22.7 %all-to-all-done = bf16[3,64,16,128]{3,2,0,1:T(8,128)(2,1)S(1)} async-done(((bf16[3,64,16,128]{3,2,0,1:T(8,128)(2,1)}), bf16[3,64,16,128]{3,2,0,1:T(8,128)(2,1)S(1)}, u32[]{:S(2)}, u32[]{:S(2)}) %all-to-all-start) | async-done | bytes 786464 | tf_op jit(solution)/shard_map/all_to_all | solution.py:34
  55.8 0.1 copy.22
  56.0 0.8 gather_fusion.2
  56.7 48.2 %all-gather.2.cloned.1.call-done = bf16[3,1024,8,128]{3,2,1,0:T(8,128)(2,1)} async-done(((bf16[3,16,8,128]{3,2,1,0:T(8,128)(2,1)}), bf16[3,1024,8,128]{3,2,1,0:T(8,128)(2,1)}) %all-gather.2.cloned.1.call-update) | async-done | bytes 6291472 | tf_op jit(solution)/shard_map/all_gather | solution.py:35
  105.0 7.4 %gather_fusion.1 = bf16[24,128,8,128]{3,2,1,0:T(8,128)(2,1)} fusion(bf16[3,8,128,8,128]{4,3,2,1,0:T(8,128)(2,1)} %bitcast.34, s32[24]{0:T(128)S(1)} %reshape.387), kind=kCustom, calls=%fused_computation.1 | custom fusion | bytes 12583104 | tf_op jit(solution)/shard_map/jit(take_along_axis)/gather | solution.py:42
  112.4 3.4 %broadcast_select_fusion = bf16[3,8,128,8,128]{4,3,2,1,0:T(8,128)(2,1)S(1)} fusion(bf16[3,8,128,8,128]{4,3,2,1,0:T(8,128)(2,1)} %bitcast.32, pred[3,8]{1,0:T(4,128)(4,1)S(1)} %fusion.17), kind=kLoop, calls=%fused_computation.5 | loop fusion | flops 3145728 | bytes 12582936 | tf_op jit(solution)/shard_map/jit(take_along_axis)/select_n | solution.py:42
  115.8 3.5 %fusion.3 = bf16[8,128,8,128]{1,3,2,0:T(8,128)(2,1)} fusion(bf16[3,8,128,8,128]{4,3,2,1,0:T(8,128)(2,1)S(1)} %broadcast_select_fusion, bf16[3,8,128,128]{3,2,1,0:T(8,128)(2,1)S(1)} %bitcast.37, pred[3,8]{1,0:T(4,128)(4,1)S(1)} %fusion.17), kind=kOutput, calls=%fused_computation.8 | convolution fusion | flops 805699584 | bytes 9175064 | tf_op jit(solution)/shard_map/kiqca,kqcjb->iqajb/dot_general | solution.py:43
  119.3 2.5 %gather_fusion = bf16[8,128,8,128]{1,3,2,0:T(8,128)(2,1)S(1)} fusion(bf16[8,128,8,128]{1,3,2,0:T(8,128)(2,1)} %fusion.3, s32[1024]{0:T(1024)S(1)} %pad_clamp_fusion), kind=kCustom, calls=%fused_computation | custom fusion | bytes 4194336 | tf_op jit(solution)/shard_map/jit(take_along_axis)/gather | solution.py:47
  121.9 2.0 fusion.6
  123.8 4.0 %copy.25 = bf16[1,8,8,128,128]{4,3,2,1,0:T(8,128)(2,1)} copy(bf16[1,8,8,128,128]{3,4,1,2,0:T(8,128)(2,1)} %fusion.6) | data formatting | bytes 4194304 | tf_op jit(solution)/shard_map/convert_element_type | solution.py:51
  127.8 37.3 %reduce-scatter.2.cloned.1.call-done = bf16[1,1,1024,128]{3,2,1,0:T(8,128)(2,1)} async-done(((bf16[1,8,1024,128]{3,2,1,0:T(8,128)(2,1)}), bf16[1,1,1024,128]{3,2,1,0:T(8,128)(2,1)}) %reduce-scatter.2.cloned.1.call-update) | async-done | bytes 262160 | tf_op jit(solution)/shard_map/reduce_scatter | solution.py:52
  165.1 27.2 %all_to_all.14 = bf16[64,16,128]{2,1,0:T(8,128)(2,1)S(1)} all-to-all(bf16[64,16,128]{2,1,0:T(8,128)(2,1)} %bitcast.38), channel_id=1, replica_groups=mesh['batch'=8,'grp'=64] {'grp'}, dimensions={0} | all-to-all | bytes 524288 | tf_op jit(solution)/shard_map/all_to_all | solution.py:54
  192.3 0.7 copy.38
  (7 shorter events, 0.1 us)
Async XLA Ops:
  6.5 98.4 %all-gather.2.cloned.1.call-start = ((), (), s32[]{:S(2)}) async-start(), calls=%async_computation.3 | async-start | bytes 6389760 | tf_op jit(solution)/shard_map/all_gather | solution.py:35
  15.4 40.4 %all-to-all-start = ((bf16[3,64,16,128]{3,2,0,1:T(8,128)(2,1)}), bf16[3,64,16,128]{3,2,0,1:T(8,128)(2,1)S(1)}, u32[]{:S(2)}, u32[]{:S(2)}) async-start(bf16[3,64,16,128]{3,2,0,1:T(8,128)(2,1)} %fusion.8), calls=%async_computation | async-start | bytes 1572864 | tf_op jit(solution)/shard_map/all_to_all | solution.py:34
  30.2 134.9 %reduce-scatter.2.cloned.1.call-start = ((), (), s32[]{:S(2)}) async-start(), calls=%async_computation.4 | async-start | bytes 2359296 | tf_op jit(solution)/shard_map/reduce_scatter | solution.py:52
Sparse Core Ops, SparseCore 0:
  11.5 93.4 all-gather.1
  127.9 37.1 reduce-scatter.1

commit v2 on v1

v2 whole, which is shorter than its diff:
```python
import jax
import jax.numpy as jnp
from jax import lax
from jax.experimental import pallas as pl
from jax.experimental.pallas import tpu as pltpu
from jax.sharding import PartitionSpec as P

MESH = pl.DeviceIdType.MESH
NX, NZ, NC = 4, 8, 2


def gather_kernel(src, out, local_sem, send, recv):
    y, g = lax.axis_index("batch"), lax.axis_index("grp")
    core = lax.rem(g, NC)
    z = lax.rem(lax.div(g, NC), NZ)
    x = lax.div(g, NC * NZ)
    other = 1 - core

    def dev(xx, zz, cc):
        return (y, (xx * NZ + zz) * NC + cc)

    def xo(d):
        return lax.rem(x + d + NX, NX)

    def zo(d):
        return lax.rem(z + d + NZ, NZ)

    half = src.shape[1] // 2
    low, high = pl.ds(0, half), pl.ds(half, half)
    used = [0]

    def copy(view, at, target):
        n = used[0]
        used[0] += 1
        c = pltpu.make_async_remote_copy(
            src_ref=view, dst_ref=at, send_sem=send.at[n], recv_sem=recv.at[n], device_id=target, device_id_type=MESH
        )
        c.start()
        return c

    partners = [dev(xo(d), z, core) for d in range(1, NX)]
    partners += [dev(x, zo(d), core) for d in range(1, NZ)]
    partners += [dev(x, z, other)]
    own = pltpu.make_async_copy(src, out.at[:, x, z, core], local_sem)
    own.start()
    barrier = pltpu.get_barrier_semaphore()
    for p in partners:
        pl.semaphore_signal(barrier, inc=1, device_id=p, device_id_type=MESH)
    pl.semaphore_wait(barrier, len(partners))

    started = []

    def go(view, at, target):
        c = copy(view, at, target)
        started.append(c)
        return c

    def same(ref, target):
        return go(ref, ref, target)

    mate = dev(x, z, other)
    along_x = [go(src.at[:, low], out.at[:, x, z, core, low], dev(xo(d), z, core)) for d in range(1, NX)]
    along_z = [go(src.at[:, high], out.at[:, x, z, core, high], dev(x, zo(d), core)) for d in range(1, NZ)]
    own.wait()

    def row(zz):
        return out.at[:, :, zz, core, low]

    def row_part(zz, part):
        return out.at[:, pl.ds(part * (NX // 2), NX // 2), zz, core, low]

    def col(xx):
        return out.at[:, xx, :, core, high]

    def col_part(xx, part):
        return out.at[:, xx, pl.ds(part * (NZ // 2), NZ // 2), core, high]

    mates = []
    zp, zm = dev(x, zo(1), core), dev(x, zo(-1), core)
    xp, xm = dev(xo(1), z, core), dev(xo(-1), z, core)
    for c in along_x:
        c.wait_recv()
    up = same(row(z), zp)
    down = same(row(z), zm)
    mates.append(same(row(z), mate))
    for c in along_z:
        c.wait_recv()
    right = same(col(x), xp)
    left = same(col(x), xm)
    mates.append(same(col(x), mate))
    for s in range(1, NZ // 2):
        last = s == NZ // 2 - 1
        up.wait_recv()
        up_next = same(row_part(zo(-s), 0) if last else row(zo(-s)), zp)
        down.wait_recv()
        down_next = same(row_part(zo(s), 1) if last else row(zo(s)), zm)
        mates.append(same(row(zo(-s)), mate))
        mates.append(same(row(zo(s)), mate))
        up, down = up_next, down_next
        if s == 2:
            right.wait_recv()
            right2 = same(col_part(xo(-1), 0), xp)
            left.wait_recv()
            left2 = same(col_part(xo(1), 1), xm)
            mates.append(same(col(xo(-1)), mate))
            mates.append(same(col(xo(1)), mate))
    right2.wait_recv()
    left2.wait_recv()
    mates.append(same(col(xo(2)), mate))
    up.wait_recv()
    down.wait_recv()
    mates.append(same(row(zo(NZ // 2)), mate))
    for c in mates:
        c.wait_recv()
    for c in started:
        c.wait_send()


COPIES = 34


def gather(block):
    k, j, c, b = block.shape
    return pl.pallas_call(
        gather_kernel,
        out_shape=jax.ShapeDtypeStruct((k, NX, NZ, NC, j, c, b), block.dtype),
        in_specs=[pl.BlockSpec(memory_space=pltpu.VMEM)],
        out_specs=pl.BlockSpec(memory_space=pl.ANY),
        scratch_shapes=[
            pltpu.SemaphoreType.DMA,
            pltpu.SemaphoreType.DMA((COPIES,)),
            pltpu.SemaphoreType.DMA((COPIES,)),
        ],
        compiler_params=pltpu.CompilerParams(collective_id=0, has_side_effects=True),
        cost_estimate=pl.CostEstimate(flops=0, bytes_accessed=12 << 20, transcendentals=0),
    )(block)


def product_kernel(flips, *refs):
    n = (len(refs) - 1) // 2
    out = refs[-1]
    lhs = jnp.concatenate([r[0, 0].reshape(-1, r.shape[-1]) for r in refs[:n]], axis=0)
    rhs = refs[n:-1]
    js = out.shape[0]
    for j in range(0, js, 2):
        cols = [
            jnp.concatenate([r[0, 0, :, jj].reshape(-1, r.shape[-1]) for r in rhs], axis=0) for jj in (j, j + 1)
        ]
        both = lax.dot_general(
            lhs, jnp.concatenate(cols, axis=1), (((0,), (0,)), ((), ())), preferred_element_type=jnp.float32
        )
        w = both.shape[1] // 2
        out[j] = both[:, :w].astype(out.dtype)
        out[j + 1] = both[:, w:].astype(out.dtype)


def product(flips, amps, inter):
    k, n, sub, c, a = amps.shape
    j, b = inter.shape[3], inter.shape[5]

    def amp_spec(kk):
        return pl.BlockSpec((1, 1, sub, c, a), lambda r, f: (kk, r ^ f[kk], 0, 0, 0))

    def inter_spec(kk):
        return pl.BlockSpec((1, 1, sub, j, c, b), lambda r, f: (kk, r ^ f[kk], 0, 0, 0, 0))

    return pl.pallas_call(
        product_kernel,
        out_shape=jax.ShapeDtypeStruct((j, n * a, b), jnp.bfloat16),
        grid_spec=pltpu.PrefetchScalarGridSpec(
            num_scalar_prefetch=1,
            grid=(n,),
            in_specs=[amp_spec(kk) for kk in range(k)] + [inter_spec(kk) for kk in range(k)],
            out_specs=pl.BlockSpec((j, a, b), lambda r, f: (0, r, 0)),
        ),
        cost_estimate=pl.CostEstimate(flops=2 * k * n * sub * c * a * j * b, bytes_accessed=9 << 20, transcendentals=0),
    )(flips, *([amps] * k), *([inter] * k))


def shards(amps, cycle_inter, k_irrep, i_irrep, j_irrep, virt_count):
    k_local = amps.shape[0]
    slab_size = amps.shape[2]
    width = amps.shape[3]
    n_irrep = virt_count.shape[0]
    j_total = cycle_inter.shape[2]
    irreps = jnp.arange(n_irrep, dtype=jnp.int32)
    slot_pos = jnp.arange(width, dtype=jnp.int32)

    def count_of(labels):
        return jnp.sum(jnp.where(labels[..., None] == irreps, virt_count, 0), axis=-1)

    grp = lax.axis_index("grp")
    k_first = lax.axis_index("batch") * k_local
    k_labels = lax.dynamic_slice_in_dim(k_irrep, k_first, k_local)
    c_label = grp * slab_size // width
    c_pos = grp * slab_size % width + jnp.arange(slab_size, dtype=jnp.int32)
    c_live = c_pos < count_of(c_label)
    a_counts = count_of(k_labels[:, None] ^ i_irrep[None, :] ^ c_label)
    amp_mask = c_live[None, None, :, None] & (slot_pos < a_counts[:, :, None, None])
    masked_amps = jnp.where(amp_mask, amps, jnp.zeros((), amps.dtype))
    b_counts = count_of(k_labels[:, None] ^ j_irrep[None, :] ^ c_label)
    inter_mask = c_live[None, None, :, None] & (slot_pos < b_counts[:, :, None, None])
    turned = jnp.transpose(cycle_inter, (0, 2, 1, 3))
    masked_inter = jnp.where(inter_mask, turned, jnp.zeros((), cycle_inter.dtype))
    sorted_amps = lax.all_to_all(masked_amps, "grp", split_axis=1, concat_axis=1, tiled=True)
    whole_inter = gather(masked_inter)
    i_label = lax.dynamic_index_in_dim(i_irrep, grp, keepdims=False)
    sub = width // slab_size
    partial = product(
        k_labels ^ i_label,
        sorted_amps.reshape(k_local, n_irrep, sub, slab_size, width),
        whole_inter.reshape(k_local, n_irrep, sub, j_total, slab_size, width),
    )
    summed = lax.psum_scatter(partial, "batch", scatter_dimension=0, tiled=True)
    outgoing = summed.reshape(-1, slab_size, width)
    arrived = lax.all_to_all(outgoing, "grp", split_axis=0, concat_axis=0, tiled=True)
    return arrived.reshape(-1, 1, slab_size, width)


def solution(mesh):
    return jax.shard_map(
        shards,
        mesh=mesh,
        in_specs=(P("batch", None, "grp", None), P("batch", "grp", None, None), P(), P(), P(), P()),
        out_specs=P(None, "batch", "grp", None),
        check_vma=False,
    )
```

time: 200 us -> 167 us (0.83)
  waiting for transfers between devices: 108 us -> 37.9 us
  Pallas kernels: 0 us -> 58.1 us
  local copies, waits for them, and re-layouts: 17.7 us -> 3.11 us
  matrix products: 3.53 us -> 0 us
  other arithmetic: 14.8 us -> 11.3 us
    pallas_call x0 -> x2, Pallas kernels: none -> 58.1 us  [the longest x1 49.7 us: gather(): pl.pallas_call(gather_kernel, out_shape=jax.ShapeDtypeStruct((k, NX, NZ,...]
    all_gather x1 -> x0, waiting for transfers between devices: 48.2 us -> none  [shards(): whole_inter = lax.all_gather(masked_inter, 'grp', axis=1, tiled=True)]
    all_to_all x1, waiting for transfers between devices: 22.7 us -> 0.01 us  [shards(): lax.all_to_all(masked_amps, 'grp', split_axis=1, concat_axis=1, tiled=True)]
    gather x4 -> x0, local copies, waits for them, and re-layouts: 10.8 us -> none  [the longest x2 7.46 us: shards(): jnp.take_along_axis(inter_blocks, k_source[:, :, None, None, None], axis=1)]
    select_n x4 -> x1, other arithmetic: 5.77 us -> 1.64 us  [shards(): jnp.where(inter_mask, turned, jnp.zeros((), cycle_inter.dtype))]
    convert_element_type x1 -> x0, local copies, waits for them, and re-layouts: 3.96 us -> none  [shards(): rounded = partial_value.astype(jnp.bfloat16)]
    dot_general x1 -> x0, matrix products: 3.53 us -> none  [shards(): jnp.einsum('kiqca,kqcjb->iqajb', amp_perm, inter_perm, preferred_element_...]
  transfers between devices with their start and end apart: 3 -> 2, of which waited for: 3 -> 1; matrix products, arithmetic and copies ran while one was open for 4% -> 2% of each run, Pallas kernels for 0% -> 30%
where the time goes in v2:
time: 167 us; the launch traced here: 166 us
  Pallas kernels  58.1 us (35%)
  waiting for transfers between devices  37.9 us (23%)
  blocking collectives  27.6 us (17%)
  starting transfers between devices  14.9 us (9%)
  between operations  13.4 us (8%)
  other arithmetic  11.3 us (7%)
  local copies, waits for them, and re-layouts  3.11 us (2%)
    pallas_call x1, Pallas kernels, gather(): pl.pallas_call(gather_kernel, out_shape=jax.ShapeDtypeStruct((k, NX, NZ,...  49.7 us
    reduce_scatter x1, waiting for transfers between devices, shards(): summed = lax.psum_scatter(partial, 'batch', scatter_dimension=0, tiled=True)  37.9 us
    all_to_all x1, blocking collectives, shards(): lax.all_to_all(outgoing, 'grp', split_axis=0, concat_axis=0, tiled=True)  27.6 us
    all_to_all x1, starting transfers between devices, shards(): lax.all_to_all(masked_amps, 'grp', split_axis=1, concat_axis=1, tiled=True)  14.8 us
    pallas_call x1, Pallas kernels, product(): pl.pallas_call(product_kernel, out_shape=jax.ShapeDtypeStruct((j, n * a,...  8.46 us
  transfers between devices with their start and end apart: 2, of which 1 were waited for; matrix products, arithmetic and copies ran while one was open for 2% of the time, Pallas kernels for 30%

profile of v2, /device:TPU:1, one launch (start us, length us, event | category | flops | bytes accessed | tf_op | source)
XLA Modules:
  0.0 166.3 jit_solution(16215029728736192036)
XLA Ops:
  6.5 1.4 fusion
  7.9 1.2 dynamic_slice.8
  9.1 1.9 %broadcast_xor_fusion = (s32[3]{0:T(128)}, s32[3]{0:T(128)S(1)}) fusion(s32[]{:T(128)} %bitcast, s32[24]{0:T(128)} %param.8, s32[]{:T(128)S(6)} %select_n.38), kind=kLoop, calls=%fused_computation.13 | loop fusion | flops 3 | bytes 44 | tf_op jit(solution)/shard_map/xor | solution.py:210
  11.0 0.7 xor_xor_fusion.1
  11.8 0.7 select_reduce_fusion.1
  12.5 0.1 copy.11
  12.6 0.1 iota_compare_fusion
  12.7 0.7 add_compare_fusion
  13.4 2.4 %and_select_fusion = bf16[3,64,16,128]{3,2,0,1:T(8,128)(2,1)} fusion(bf16[3,64,16,128]{3,2,1,0:T(8,128)(2,1)} %param.6, pred[3,64,128]{2,0,1:T(4,128)(4,1)S(1)} %iota_compare_fusion, pred[16]{0:T(512)(128)(4,1)S(1)} %add_compare_fusion), kind=kLoop, calls=%fused_computation | loop fusion | flops 786432 | bytes 1597456 | tf_op jit(solution)/shard_map/jit(_where)/select_n | solution.py:200
  15.9 14.8 %all-to-all-start = ((bf16[3,64,16,128]{3,2,0,1:T(8,128)(2,1)}), bf16[3,64,16,128]{3,2,0,1:T(8,128)(2,1)S(1)}, u32[]{:S(2)}, u32[]{:S(2)}) async-start(bf16[3,64,16,128]{3,2,0,1:T(8,128)(2,1)} %and_select_fusion), calls=%async_computation | async-start | bytes 1572864 | tf_op jit(solution)/shard_map/all_to_all | solution.py:205
  30.7 0.0 reduce-scatter.2.cloned.1.call-start
  30.7 0.7 xor_xor_fusion
  31.5 0.9 select_reduce_fusion
  32.3 0.1 iota_compare_fusion.2
  32.4 1.6 and_select_fusion.1.src
  34.1 49.7 %shard_map.64 = bf16[3,4,8,2,8,16,128]{6,5,4,3,2,1,0:T(8,128)(2,1)} custom-call(bf16[3,8,16,128]{3,2,1,0:T(8,128)(2,1)} %and_select_fusion.1.src), custom_call_target="tpu_custom_call" | custom-call | bytes 12582912 | tf_op jit(solution)/shard_map/pallas_call | solution.py:124
  83.7 0.0 all-to-all-done
  83.7 1.1 copy.13
  84.8 8.5 %shard_map.65 = bf16[8,1024,128]{2,1,0:T(8,128)(2,1)} custom-call(s32[3]{0:T(128)} %get-tuple-element.5.flips, bf16[3,8,8,16,128]{4,3,2,1,0:T(8,128)(2,1)} %bitcast.10, bf16[3,8,8,16,128]{4,3,2,1,0:T(8,128)(2,1)} %bitcast.11, bf16[3,8,8,16,128]{4,3,2,1,0:T(8,128)(2,1)} %bitcast.12, bf16[3,8,8,8,16,128]{5,4,3,2,1,0:T(8,128)(2,1)} %bitcast.7, ...), custom_call_target="tpu_custom_call" | custom-call | flops 805306368 | bytes 9437184 | tf_op jit(solution)/shard_map/pallas_call | solution.py:167
  93.3 0.0 reduce-scatter.2.cloned.1.call-update
  93.3 37.9 %reduce-scatter.2.cloned.1.call-done = bf16[1,1024,128]{2,1,0:T(8,128)(2,1)} async-done(((bf16[8,1024,128]{2,1,0:T(8,128)(2,1)}), bf16[1,1024,128]{2,1,0:T(8,128)(2,1)}) %reduce-scatter.2.cloned.1.call-update) | async-done | bytes 262160 | tf_op jit(solution)/shard_map/reduce_scatter | solution.py:214
  131.2 27.6 %all_to_all.10 = bf16[64,16,128]{2,1,0:T(8,128)(2,1)S(1)} all-to-all(bf16[64,16,128]{2,1,0:T(8,128)(2,1)} %bitcast.14), channel_id=1, replica_groups=mesh['batch'=8,'grp'=64] {'grp'}, dimensions={0} | all-to-all | bytes 524288 | tf_op jit(solution)/shard_map/all_to_all | solution.py:216
  158.8 0.7 copy.18
Async XLA Ops:
  15.9 67.9 %all-to-all-start = ((bf16[3,64,16,128]{3,2,0,1:T(8,128)(2,1)}), bf16[3,64,16,128]{3,2,0,1:T(8,128)(2,1)S(1)}, u32[]{:S(2)}, u32[]{:S(2)}) async-start(bf16[3,64,16,128]{3,2,0,1:T(8,128)(2,1)} %and_select_fusion), calls=%async_computation | async-start | bytes 1572864 | tf_op jit(solution)/shard_map/all_to_all | solution.py:205
  30.7 100.5 %reduce-scatter.2.cloned.1.call-start = ((), (), s32[]{:S(2)}) async-start(), calls=%async_computation.3 | async-start | bytes 2359296 | tf_op jit(solution)/shard_map/reduce_scatter | solution.py:214
Sparse Core Ops, SparseCore 0:
  93.4 37.7 reduce-scatter.1

commit v3 on v2

--- a/solution.py
+++ b/solution.py
@@ -136,85 +136,171 @@
     )(block)
 
 
-def product_kernel(flips, *refs):
-    n = (len(refs) - 1) // 2
-    out = refs[-1]
-    lhs = jnp.concatenate([r[0, 0].reshape(-1, r.shape[-1]) for r in refs[:n]], axis=0)
-    rhs = refs[n:-1]
-    js = out.shape[0]
-    for j in range(0, js, 2):
-        cols = [
-            jnp.concatenate([r[0, 0, :, jj].reshape(-1, r.shape[-1]) for r in rhs], axis=0) for jj in (j, j + 1)
-        ]
-        both = lax.dot_general(
-            lhs, jnp.concatenate(cols, axis=1), (((0,), (0,)), ((), ())), preferred_element_type=jnp.float32
+def reduce_kernel(k_irrep, i_irrep, j_irrep, counts, amps, inter, out, lhs, part, to_up, at_up, to_down, at_down, *sems):
+    send_up, recv_up, send_down, recv_down = sems
+    y, g = lax.axis_index("batch"), lax.axis_index("grp")
+    n, _, ks, c, a = amps.shape
+    rows = amps.shape[1] * c
+    ring = inter.shape[3]
+    far = ring // 2
+    b = inter.shape[5]
+    per = n // 2
+
+    def yo(d):
+        return lax.rem(y + d + ring, ring)
+
+    barrier = pltpu.get_barrier_semaphore()
+    for d in (1, -1):
+        pl.semaphore_signal(barrier, inc=1, device_id=(yo(d), g), device_id_type=MESH)
+
+    i_label = i_irrep[g]
+    flips = [k_irrep[y * ks + kk] ^ i_label for kk in range(ks)]
+    c_pos = lax.broadcasted_iota(jnp.int32, (rows, a), 0)
+
+    def prepare(r, carry):
+        for kk in range(ks):
+            irrep = r ^ flips[kk]
+            block = amps[irrep, :, kk].reshape(rows, a).astype(jnp.float32)
+            live = jnp.where(c_pos < counts[irrep], block, 0.0)
+            lhs[r, :, kk * rows : (kk + 1) * rows] = live.T.astype(lhs.dtype)
+        return carry
+
+    lax.fori_loop(0, n, prepare, 0)
+
+    def right(r, j):
+        return jnp.concatenate([inter[kk, r ^ flips[kk], :, j].reshape(rows, b) for kk in range(ks)], axis=0)
+
+    def one(r, j):
+        return jnp.dot(lhs[r], right(r, j), preferred_element_type=jnp.float32)
+
+    def two(r, j, jj):
+        both = jnp.concatenate([right(r, j), right(r, jj)], axis=1)
+        return jnp.dot(lhs[r], both, preferred_element_type=jnp.float32)
+
+    ups, downs = {}, {}
+
+    def send(table, src, dst, send_sem, recv_sem, s, h, step):
+        copy = pltpu.make_async_remote_copy(
+            src_ref=src.at[s, h],
+            dst_ref=dst.at[s, h],
+            send_sem=send_sem.at[s, h],
+            recv_sem=recv_sem.at[s, h],
+            device_id=(yo(step), g),
+            device_id_type=MESH,
         )
-        w = both.shape[1] // 2
-        out[j] = both[:, :w].astype(out.dtype)
-        out[j + 1] = both[:, w:].astype(out.dtype)
-
-
-def product(flips, amps, inter):
-    k, n, sub, c, a = amps.shape
+        copy.start()
+        table[s, h] = copy
+
+    def send_upward(s, h):
+        send(ups, to_up, at_up, send_up, recv_up, s, h, 1)
+
+    def send_downward(s, h):
+        send(downs, to_down, at_down, send_down, recv_down, s, h, -1)
+
+    def first(r, carry):
+        to_up[0, 0, r] = one(r, yo(far)).astype(to_up.dtype)
+        return carry
+
+    def second(r, carry):
+        to_down[0, 1, r] = one(r + per, yo(far)).astype(to_down.dtype)
+        return carry
+
+    lax.fori_loop(0, per, first, 0)
+    pl.semaphore_wait(barrier, 2)
+    send_upward(0, 0)
+    lax.fori_loop(0, per, second, 0)
+    send_downward(0, 1)
+
+    for s in range(1, far):
+
+        def products(r, carry):
+            both = two(r, yo(far - s), yo(s - far))
+            part[0, r] = both[:, :b]
+            part[1, r] = both[:, b:]
+            return carry
+
+        lax.fori_loop(0, n, products, 0)
+
+        def upward(h):
+            value = part[0, pl.ds(h * per, per)]
+            if (s - 1, h) in ups:
+                ups[s - 1, h].wait_recv()
+                value = value + at_up[s - 1, h].astype(jnp.float32)
+            to_up[s, h] = value.astype(to_up.dtype)
+            send_upward(s, h)
+
+        def downward(h):
+            value = part[1, pl.ds(h * per, per)]
+            if (s - 1, h) in downs:
+                downs[s - 1, h].wait_recv()
+                value = value + at_down[s - 1, h].astype(jnp.float32)
+            to_down[s, h] = value.astype(to_down.dtype)
+            send_downward(s, h)
+
+        order = (1, 0) if s == 1 else (0, 1)
+        for h in order:
+            upward(h)
+            downward(1 - h if s == 1 else h)
+
+    def own(r, carry):
+        part[0, r] = one(r, y)
+        return carry
+
+    lax.fori_loop(0, n, own, 0)
+    flip = i_label ^ j_irrep[y]
+    a_pos = lax.broadcasted_iota(jnp.int32, (a, b), 0)
+    b_pos = lax.broadcasted_iota(jnp.int32, (a, b), 1)
+    for h in (1, 0):
+        ups[far - 1, h].wait_recv()
+        downs[far - 1, h].wait_recv()
+
+        def total(r, carry):
+            irrep = r + h * per
+            value = part[0, irrep] + at_up[far - 1, h, r].astype(jnp.float32) + at_down[far - 1, h, r].astype(jnp.float32)
+            live = (a_pos < counts[irrep]) & (b_pos < counts[irrep ^ flip])
+            out[irrep] = jnp.where(live, value, 0.0).astype(out.dtype)
+            return carry
+
+        lax.fori_loop(0, per, total, 0)
+    for copy in list(ups.values()) + list(downs.values()):
+        copy.wait_send()
+
+
+def reduce(amps, inter, k_irrep, i_irrep, j_irrep, counts):
+    n, sub, k, c, a = amps.shape
     j, b = inter.shape[3], inter.shape[5]
-
-    def amp_spec(kk):
-        return pl.BlockSpec((1, 1, sub, c, a), lambda r, f: (kk, r ^ f[kk], 0, 0, 0))
-
-    def inter_spec(kk):
-        return pl.BlockSpec((1, 1, sub, j, c, b), lambda r, f: (kk, r ^ f[kk], 0, 0, 0, 0))
-
+    half = (j // 2, 2, n // 2, a, b)
     return pl.pallas_call(
-        product_kernel,
-        out_shape=jax.ShapeDtypeStruct((j, n * a, b), jnp.bfloat16),
-        grid_spec=pltpu.PrefetchScalarGridSpec(
-            num_scalar_prefetch=1,
-            grid=(n,),
-            in_specs=[amp_spec(kk) for kk in range(k)] + [inter_spec(kk) for kk in range(k)],
-            out_specs=pl.BlockSpec((j, a, b), lambda r, f: (0, r, 0)),
-        ),
+        reduce_kernel,
+        out_shape=jax.ShapeDtypeStruct((n, a, b), jnp.bfloat16),
+        in_specs=[pl.BlockSpec(memory_space=pltpu.SMEM)] * 4 + [pl.BlockSpec(memory_space=pltpu.VMEM)] * 2,
+        out_specs=pl.BlockSpec(memory_space=pltpu.VMEM),
+        scratch_shapes=[pltpu.VMEM((n, a, k * sub * c), jnp.bfloat16), pltpu.VMEM((2, n, a, b), jnp.float32)]
+        + [pltpu.VMEM(half, jnp.bfloat16)] * 4
+        + [pltpu.SemaphoreType.DMA(half[:2])] * 4,
+        compiler_params=pltpu.CompilerParams(collective_id=1, has_side_effects=True, vmem_limit_bytes=48 << 20),
         cost_estimate=pl.CostEstimate(flops=2 * k * n * sub * c * a * j * b, bytes_accessed=9 << 20, transcendentals=0),
-    )(flips, *([amps] * k), *([inter] * k))
+    )(k_irrep, i_irrep, j_irrep, counts, amps, inter)
 
 
 def shards(amps, cycle_inter, k_irrep, i_irrep, j_irrep, virt_count):
-    k_local = amps.shape[0]
-    slab_size = amps.shape[2]
-    width = amps.shape[3]
+    k_local, i_total, slab_size, width = amps.shape
     n_irrep = virt_count.shape[0]
     j_total = cycle_inter.shape[2]
-    irreps = jnp.arange(n_irrep, dtype=jnp.int32)
-    slot_pos = jnp.arange(width, dtype=jnp.int32)
-
-    def count_of(labels):
-        return jnp.sum(jnp.where(labels[..., None] == irreps, virt_count, 0), axis=-1)
-
-    grp = lax.axis_index("grp")
-    k_first = lax.axis_index("batch") * k_local
-    k_labels = lax.dynamic_slice_in_dim(k_irrep, k_first, k_local)
-    c_label = grp * slab_size // width
-    c_pos = grp * slab_size % width + jnp.arange(slab_size, dtype=jnp.int32)
-    c_live = c_pos < count_of(c_label)
-    a_counts = count_of(k_labels[:, None] ^ i_irrep[None, :] ^ c_label)
-    amp_mask = c_live[None, None, :, None] & (slot_pos < a_counts[:, :, None, None])
-    masked_amps = jnp.where(amp_mask, amps, jnp.zeros((), amps.dtype))
-    b_counts = count_of(k_labels[:, None] ^ j_irrep[None, :] ^ c_label)
-    inter_mask = c_live[None, None, :, None] & (slot_pos < b_counts[:, :, None, None])
-    turned = jnp.transpose(cycle_inter, (0, 2, 1, 3))
-    masked_inter = jnp.where(inter_mask, turned, jnp.zeros((), cycle_inter.dtype))
-    sorted_amps = lax.all_to_all(masked_amps, "grp", split_axis=1, concat_axis=1, tiled=True)
-    whole_inter = gather(masked_inter)
-    i_label = lax.dynamic_index_in_dim(i_irrep, grp, keepdims=False)
     sub = width // slab_size
-    partial = product(
-        k_labels ^ i_label,
-        sorted_amps.reshape(k_local, n_irrep, sub, slab_size, width),
+    sorted_amps = lax.all_to_all(jnp.transpose(amps, (1, 0, 2, 3)), "grp", split_axis=0, concat_axis=0, tiled=True)
+    whole_inter = gather(jnp.transpose(cycle_inter, (0, 2, 1, 3)))
+    summed = reduce(
+        sorted_amps.reshape(n_irrep, sub, k_local, slab_size, width),
         whole_inter.reshape(k_local, n_irrep, sub, j_total, slab_size, width),
+        k_irrep,
+        i_irrep,
+        j_irrep,
+        virt_count,
     )
-    summed = lax.psum_scatter(partial, "batch", scatter_dimension=0, tiled=True)
-    outgoing = summed.reshape(-1, slab_size, width)
+    outgoing = summed.reshape(i_total, slab_size, width)
     arrived = lax.all_to_all(outgoing, "grp", split_axis=0, concat_axis=0, tiled=True)
-    return arrived.reshape(-1, 1, slab_size, width)
+    return arrived.reshape(i_total, 1, slab_size, width)
 
 
 def solution(mesh):

time: 167 us -> 121 us (0.72)
  waiting for transfers between devices: 37.9 us -> 0.01 us
  Pallas kernels: 58.1 us -> 82.1 us
  between operations: 13.4 us -> 0.08 us
  other arithmetic: 11.3 us -> 0 us
  blocking collectives: 27.6 us -> 19.6 us
    reduce_scatter x1 -> x0, waiting for transfers between devices: 37.9 us -> none  [shards(): summed = lax.psum_scatter(partial, 'batch', scatter_dimension=0, tiled=True)]
    pallas_call x1, Pallas kernels: 8.46 us -> 30.6 us  [reduce(): pl.pallas_call(reduce_kernel, out_shape=jax.ShapeDtypeStruct((n, a, b), j...]
    all_to_all x1, blocking collectives: 27.6 us -> 19.6 us  [shards(): lax.all_to_all(outgoing, 'grp', split_axis=0, concat_axis=0, tiled=True)]
    select_n x2 -> x0, other arithmetic: 4.05 us -> none  [the longest x1 2.41 us: shards(): masked_amps = jnp.where(amp_mask, amps, jnp.zeros((), amps.dtype))]
    unnamed x1 -> x11, local copies, waits for them, and re-layouts: 0.7 us -> 4.46 us
    xor x3 -> x0, other arithmetic: 3.35 us -> none  [the longest x1 1.89 us: shards(): k_labels ^ i_label]
    reduce_sum x3 -> x0, other arithmetic: 2.98 us -> none  [count_of(): jnp.sum(jnp.where(labels[..., None] == irreps, virt_count, 0), axis=-1)]
    pallas_call x1, Pallas kernels: 49.7 us -> 51.5 us  [gather(): pl.pallas_call(gather_kernel, out_shape=jax.ShapeDtypeStruct((k, NX, NZ,...]
  transfers between devices with their start and end apart: 2 -> 1, of which waited for: 1 -> 0; matrix products, arithmetic and copies ran while one was open for 2% -> 1% of each run, Pallas kernels for 30% -> 43%
where the time goes in v3:
time: 121 us
  Pallas kernels  82.1 us (68%)
  blocking collectives  19.6 us (16%)
  starting transfers between devices  14.8 us (12%)
  local copies, waits for them, and re-layouts  4.46 us (4%)
    pallas_call x1, Pallas kernels, gather(): pl.pallas_call(gather_kernel, out_shape=jax.ShapeDtypeStruct((k, NX, NZ,...  51.5 us
    pallas_call x1, Pallas kernels, reduce(): pl.pallas_call(reduce_kernel, out_shape=jax.ShapeDtypeStruct((n, a, b), j...  30.6 us
    all_to_all x1, blocking collectives, shards(): lax.all_to_all(outgoing, 'grp', split_axis=0, concat_axis=0, tiled=True)  19.6 us
    all_to_all x1, starting transfers between devices, shards(): lax.all_to_all(jnp.transpose(amps, (1, 0, 2, 3)), 'grp', split_axis=0, co...  14.8 us
    unnamed x11, local copies, waits for them, and re-layouts  4.46 us
  transfers between devices with their start and end apart: 1, of which 0 were waited for; matrix products, arithmetic and copies ran while one was open for 1% of the time, Pallas kernels for 43%

profile of v3, /device:TPU:1, one launch (start us, length us, event | category | flops | bytes accessed | tf_op | source)
XLA Modules:
  0.0 121.0 jit_solution(11141434278958862211)
XLA Ops:
  0.0 0.0 copy-start.3
  0.0 0.0 copy-start.2
  0.0 0.0 copy-start.1
  0.0 0.0 copy-start
  0.0 2.2 %copy.13 = bf16[3,64,16,128]{3,2,0,1:T(8,128)(2,1)} copy(bf16[3,64,16,128]{3,2,1,0:T(8,128)(2,1)} %param.6) | data formatting | bytes 1572864 | tf_op args[0]
  2.2 14.8 %all-to-all-start = ((bf16[64,3,16,128]{3,2,1,0:T(8,128)(2,1)}), bf16[64,3,16,128]{3,2,1,0:T(8,128)(2,1)S(1)}, u32[]{:S(2)}, u32[]{:S(2)}) async-start(bf16[64,3,16,128]{3,2,1,0:T(8,128)(2,1)} %bitcast.8), calls=%async_computation | async-start | bytes 1572864 | tf_op jit(solution)/shard_map/all_to_all | solution.py:291
  17.0 1.5 %copy.14 = bf16[3,16,8,128]{3,1,2,0:T(8,128)(2,1)} copy(bf16[3,16,8,128]{3,2,1,0:T(8,128)(2,1)} %param.7) | data formatting | bytes 196608 | tf_op args[1]
  18.6 51.5 %shard_map.64 = bf16[3,4,8,2,8,16,128]{6,5,4,3,2,1,0:T(8,128)(2,1)} custom-call(bf16[3,8,16,128]{3,2,1,0:T(8,128)(2,1)} %bitcast.14), custom_call_target="tpu_custom_call" | custom-call | bytes 12582912 | tf_op jit(solution)/shard_map/pallas_call | solution.py:124
  70.1 0.0 all-to-all-done
  70.1 0.0 copy-done.3
  70.1 0.0 copy-done.2
  70.1 0.0 copy-done.1
  70.1 0.0 copy-done
  70.1 30.6 %shard_map.65 = bf16[8,128,128]{2,1,0:T(8,128)(2,1)S(1)} custom-call(s32[24]{0:T(128)S(1)} %copy-done, s32[64]{0:T(128)S(1)} %copy-done.1, s32[8]{0:T(128)S(1)} %copy-done.2, s32[8]{0:T(128)S(1)} %copy-done.3, bf16[8,8,3,16,128]{4,3,2,1,0:T(8,128)(2,1)S(1)} %bitcast.10, bf16[3,8,8,8,16,128]{5,4,3,2,1,0:T(8,128)(2,1)} %bitcast.12), custom_call_target="tpu_custom_call" | custom-call | flops 805306368 | bytes 9437184 | tf_op jit(solution)/shard_map/pallas_call | solution.py:273
  100.7 19.6 %all_to_all.10 = bf16[64,16,128]{2,1,0:T(8,128)(2,1)S(1)} all-to-all(bf16[64,16,128]{2,1,0:T(8,128)(2,1)S(1)} %bitcast.11), channel_id=1, replica_groups=mesh['batch'=8,'grp'=64] {'grp'}, dimensions={0} | all-to-all | bytes 524288 | tf_op jit(solution)/shard_map/all_to_all | solution.py:302
  120.3 0.7 copy.16
Async XLA Ops:
  0.0 70.1 %copy-start.3 = (s32[8]{0:T(128)S(1)}, s32[8]{0:T(128)}, u32[]{:S(2)}) copy-start(s32[8]{0:T(128)} %counts.1) | copy-start | bytes 100
  0.0 70.1 %copy-start.2 = (s32[8]{0:T(128)S(1)}, s32[8]{0:T(128)}, u32[]{:S(2)}) copy-start(s32[8]{0:T(128)} %j_irrep.1) | copy-start | bytes 100
  0.0 70.1 %copy-start.1 = (s32[64]{0:T(128)S(1)}, s32[64]{0:T(128)}, u32[]{:S(2)}) copy-start(s32[64]{0:T(128)} %i_irrep.1) | copy-start | bytes 772
  0.0 70.1 %copy-start = (s32[24]{0:T(128)S(1)}, s32[24]{0:T(128)}, u32[]{:S(2)}) copy-start(s32[24]{0:T(128)} %k_irrep.1) | copy-start | bytes 292
  2.2 67.9 %all-to-all-start = ((bf16[64,3,16,128]{3,2,1,0:T(8,128)(2,1)}), bf16[64,3,16,128]{3,2,1,0:T(8,128)(2,1)S(1)}, u32[]{:S(2)}, u32[]{:S(2)}) async-start(bf16[64,3,16,128]{3,2,1,0:T(8,128)(2,1)} %bitcast.8), calls=%async_computation | async-start | bytes 1572864 | tf_op jit(solution)/shard_map/all_to_all | solution.py:291

commit v4 on v1

v4 whole, which is shorter than its diff:
```python
import jax
import jax.numpy as jnp
from jax import lax
from jax.experimental import pallas as pl
from jax.experimental.pallas import tpu as pltpu
from jax.sharding import PartitionSpec as P

MESH = pl.DeviceIdType.MESH
NX, NZ, NC = 4, 8, 2
GRP = NX * NZ * NC
COPIES = 34


def cycle_kernel(
    k_irrep, i_irrep, j_irrep, counts, amps, src, out,
    low0, low1, low2, low3, high0, high1, high2, high3, sorted_amps, lhs, part, summed, to_up, at_up, to_down, at_down,
    local_sem, send, recv, amp_send, amp_recv, out_send, out_recv, send_up, recv_up, send_down, recv_down,
):
    y, g = lax.axis_index("batch"), lax.axis_index("grp")
    core = lax.rem(g, NC)
    z = lax.rem(lax.div(g, NC), NZ)
    x = lax.div(g, NC * NZ)
    lows, highs = (low0, low1, low2, low3), (high0, high1, high2, high3)
    _, _, _, ks, c, b = low0.shape
    ring = src.shape[0]
    far = ring // 2
    n, a = lhs.shape[:2]
    rows = lhs.shape[2] // ks
    subs = rows // c
    per = n // 2

    def yo(d):
        return lax.rem(y + d + ring, ring)

    def xo(d):
        return lax.rem(x + d + NX, NX)

    def zo(d):
        return lax.rem(z + d + NZ, NZ)

    def dev(xx, zz, cc):
        return (y, (xx * NZ + zz) * NC + cc)

    def low(t):
        return yo(far - t)

    def high(t):
        return y if t == 0 else yo(t - far)

    own_blocks = []
    for t in range(far):
        for side, (j, held) in enumerate(((low(t), lows[t]), (high(t), highs[t]))):
            own_blocks.append(pltpu.make_async_copy(src.at[j], held.at[x, z, core], local_sem.at[2 * t + side]))
    own_amps = pltpu.make_async_copy(amps.at[:, g], sorted_amps.at[g], local_sem.at[ring])
    for copy in own_blocks + [own_amps]:
        copy.start()

    barrier = pltpu.get_barrier_semaphore()

    def greet(d, carry):
        pl.semaphore_signal(barrier, inc=1, device_id=(y, lax.rem(g + d, GRP)), device_id_type=MESH)
        return carry

    lax.fori_loop(1, GRP, greet, 0)
    for d in (1, -1):
        pl.semaphore_signal(barrier, inc=1, device_id=(yo(d), g), device_id_type=MESH)
    pl.semaphore_wait(barrier, GRP + 1)

    started = []

    def go(t, view, at, target):
        table = [p for p in started if p[0] == t]
        at_sem = t * COPIES + len(table)
        copy = pltpu.make_async_remote_copy(
            src_ref=view, dst_ref=at, send_sem=send.at[at_sem], recv_sem=recv.at[at_sem], device_id=target, device_id_type=MESH
        )
        copy.start()
        started.append((t, copy))
        return copy

    def same(t, ref, target):
        return go(t, ref, ref, target)

    def row(t, zz):
        return lows[t].at[:, zz, core]

    def row_part(t, zz, p):
        return lows[t].at[pl.ds(p * (NX // 2), NX // 2), zz, core]

    def col(t, xx):
        return highs[t].at[xx, :, core]

    def col_part(t, xx, p):
        return highs[t].at[xx, pl.ds(p * (NZ // 2), NZ // 2), core]

    mate = dev(x, z, 1 - core)
    zp, zm = dev(x, zo(1), core), dev(x, zo(-1), core)
    xp, xm = dev(xo(1), z, core), dev(xo(-1), z, core)
    state = {}

    def open_chunk(t):
        along_x = [go(t, src.at[low(t)], lows[t].at[x, z, core], dev(xo(d), z, core)) for d in range(1, NX)]
        along_z = [go(t, src.at[high(t)], highs[t].at[x, z, core], dev(x, zo(d), core)) for d in range(1, NZ)]
        state[t] = dict(along_x=along_x, along_z=along_z, mates=[])

    def advance(t, step):
        st = state[t]
        mates = st["mates"]
        if step == 1:
            for copy in st["along_x"]:
                copy.wait_recv()
            st["up"] = same(t, row(t, z), zp)
            st["down"] = same(t, row(t, z), zm)
            for copy in st["along_z"]:
                copy.wait_recv()
            st["right"] = same(t, col(t, x), xp)
            st["left"] = same(t, col(t, x), xm)
            mates.append(same(t, row(t, z), mate))
            mates.append(same(t, col(t, x), mate))
        elif step <= NZ // 2:
            s = step - 1
            last = s == NZ // 2 - 1
            st["up"].wait_recv()
            up = same(t, row_part(t, zo(-s), 0) if last else row(t, zo(-s)), zp)
            st["down"].wait_recv()
            down = same(t, row_part(t, zo(s), 1) if last else row(t, zo(s)), zm)
            mates.append(same(t, row(t, zo(-s)), mate))
            mates.append(same(t, row(t, zo(s)), mate))
            st["up"], st["down"] = up, down
            if s == 2:
                st["right"].wait_recv()
                right = same(t, col_part(t, xo(-1), 0), xp)
                st["left"].wait_recv()
                left = same(t, col_part(t, xo(1), 1), xm)
                mates.append(same(t, col(t, xo(-1)), mate))
                mates.append(same(t, col(t, xo(1)), mate))
                st["right"], st["left"] = right, left
        else:
            st["right"].wait_recv()
            st["left"].wait_recv()
            mates.append(same(t, col(t, xo(2)), mate))
            st["up"].wait_recv()
            st["down"].wait_recv()
            mates.append(same(t, row(t, zo(NZ // 2)), mate))

    def close_chunk(t):
        for copy in state[t]["mates"]:
            copy.wait_recv()

    def amp_copy(d):
        target = lax.rem(g + d, GRP)
        return pltpu.make_async_remote_copy(
            src_ref=amps.at[:, target],
            dst_ref=sorted_amps.at[g],
            send_sem=amp_send.at[d],
            recv_sem=amp_recv.at[d],
            device_id=(y, target),
            device_id_type=MESH,
        )

    def start_amps(d, carry):
        amp_copy(d).start()
        return carry

    def wait_amps(d, carry):
        amp_copy(d).wait_recv()
        return carry

    def wait_amps_sent(d, carry):
        amp_copy(d).wait_send()
        return carry

    i_label = i_irrep[g]
    flips = [k_irrep[y * ks + kk] ^ i_label for kk in range(ks)]
    c_pos = lax.broadcasted_iota(jnp.int32, (rows, a), 0)

    def prepare(r, carry):
        for kk in range(ks):
            irrep = r ^ flips[kk]
            block = sorted_amps[pl.ds(irrep * subs, subs), kk].reshape(rows, a).astype(jnp.float32)
            live = jnp.where(c_pos < counts[irrep], block, 0.0)
            lhs[r, :, kk * rows : (kk + 1) * rows] = live.T.astype(lhs.dtype)
        return carry

    wide = NX * NZ * NC // n // NC
    split = NZ // wide

    def piece(r, held, kk):
        irrep = r ^ flips[kk]
        block = held[lax.div(irrep, split), pl.ds(lax.rem(irrep, split) * wide, wide), :, kk]
        return block.reshape(rows, b)

    def right_of(r, held):
        return jnp.concatenate([piece(r, held, kk) for kk in range(ks)], axis=0)

    def one(r, held):
        return jnp.dot(lhs[r], right_of(r, held), preferred_element_type=jnp.float32)

    def two(r, first, second):
        both = jnp.concatenate([right_of(r, first), right_of(r, second)], axis=1)
        return jnp.dot(lhs[r], both, preferred_element_type=jnp.float32)

    ups, downs = {}, {}

    def pass_on(table, source, dest, send_sem, recv_sem, s, h, step):
        copy = pltpu.make_async_remote_copy(
            src_ref=source.at[s, h],
            dst_ref=dest.at[s, h],
            send_sem=send_sem.at[s, h],
            recv_sem=recv_sem.at[s, h],
            device_id=(yo(step), g),
            device_id_type=MESH,
        )
        copy.start()
        table[s, h] = copy

    def upward(s, h):
        value = part[0, pl.ds(h * per, per)]
        if (s - 1, h) in ups:
            ups[s - 1, h].wait_recv()
            value = value + at_up[s - 1, h].astype(jnp.float32)
        to_up[s, h] = value.astype(to_up.dtype)
        pass_on(ups, to_up, at_up, send_up, recv_up, s, h, 1)

    def downward(s, h):
        value = part[1, pl.ds(h * per, per)]
        if (s - 1, h) in downs:
            downs[s - 1, h].wait_recv()
            value = value + at_down[s - 1, h].astype(jnp.float32)
        to_down[s, h] = value.astype(to_down.dtype)
        pass_on(downs, to_down, at_down, send_down, recv_down, s, h, -1)

    def products(s):
        def body(r, carry):
            both = two(r, lows[s], highs[s])
            part[0, r] = both[:, :b]
            part[1, r] = both[:, b:]
            return carry

        def body_one(r, carry):
            to_up[0, 0, r] = one(r, low0).astype(to_up.dtype)
            return carry

        def body_other(r, carry):
            to_down[0, 1, r] = one(r + per, low0).astype(to_down.dtype)
            return carry

        if s == 0:
            lax.fori_loop(0, per, body_one, 0)
            pass_on(ups, to_up, at_up, send_up, recv_up, 0, 0, 1)
            lax.fori_loop(0, per, body_other, 0)
            pass_on(downs, to_down, at_down, send_down, recv_down, 0, 1, -1)
            return
        lax.fori_loop(0, n, body, 0)
        for h in (1, 0) if s == 1 else (0, 1):
            upward(s, h)
            downward(s, 1 - h if s == 1 else h)

    open_chunk(0)
    lax.fori_loop(1, GRP, start_amps, 0)
    for t in range(1, far):
        open_chunk(t)
    for copy in own_blocks:
        copy.wait()
    steps = NZ // 2 + 1
    for turn in range(1, steps + far):
        if turn == steps:
            own_amps.wait()
            lax.fori_loop(1, GRP, wait_amps, 0)
            lax.fori_loop(0, n, prepare, 0)
        for t in range(far):
            if 1 <= turn - t <= steps:
                advance(t, turn - t)
        t = turn - steps - 1
        if t >= 0:
            close_chunk(t)
            products(t)
    close_chunk(far - 1)
    products(far - 1)

    def own(r, carry):
        part[0, r] = one(r, high0)
        return carry

    lax.fori_loop(0, n, own, 0)
    flip = i_label ^ j_irrep[y]
    a_pos = lax.broadcasted_iota(jnp.int32, (a, b), 0)
    b_pos = lax.broadcasted_iota(jnp.int32, (a, b), 1)
    for h in (0, 1):
        ups[far - 1, h].wait_recv()
        downs[far - 1, h].wait_recv()

        def total(r, carry):
            irrep = r + h * per
            value = part[0, irrep] + at_up[far - 1, h, r].astype(jnp.float32) + at_down[far - 1, h, r].astype(jnp.float32)
            live = (a_pos < counts[irrep]) & (b_pos < counts[irrep ^ flip])
            masked = jnp.where(live, value, 0.0).astype(summed.dtype)
            summed[pl.ds(irrep * subs, subs)] = masked.reshape(subs, c, b)
            return carry

        lax.fori_loop(0, per, total, 0)

    def out_copy(d):
        target = lax.rem(g + d, GRP)
        return pltpu.make_async_remote_copy(
            src_ref=summed.at[target],
            dst_ref=out.at[g],
            send_sem=out_send.at[d],
            recv_sem=out_recv.at[d],
            device_id=(y, target),
            device_id_type=MESH,
        )

    def start_out(d, carry):
        out_copy(d).start()
        return carry

    def wait_out(d, carry):
        out_copy(d).wait_recv()
        out_copy(d).wait_send()
        return carry

    lax.fori_loop(1, GRP, start_out, 0)
    own_out = pltpu.make_async_copy(summed.at[g], out.at[g], local_sem.at[0])
    own_out.start()
    lax.fori_loop(1, GRP, wait_amps_sent, 0)
    for _, copy in started:
        copy.wait_send()
    for copy in list(ups.values()) + list(downs.values()):
        copy.wait_send()
    own_out.wait()
    lax.fori_loop(1, GRP, wait_out, 0)


def shards(amps, cycle_inter, k_irrep, i_irrep, j_irrep, virt_count):
    ks, i_total, c, a = amps.shape
    j, b = cycle_inter.shape[2:]
    n = virt_count.shape[0]
    half = (j // 2, 2, n // 2, a, b)
    turned = jnp.transpose(cycle_inter, (2, 0, 1, 3))
    dma = pltpu.SemaphoreType.DMA
    out = pl.pallas_call(
        cycle_kernel,
        out_shape=jax.ShapeDtypeStruct((i_total, c, b), jnp.bfloat16),
        in_specs=[pl.BlockSpec(memory_space=pltpu.SMEM)] * 4
        + [pl.BlockSpec(memory_space=pl.ANY), pl.BlockSpec(memory_space=pltpu.VMEM)],
        out_specs=pl.BlockSpec(memory_space=pl.ANY),
        scratch_shapes=[pltpu.VMEM((NX, NZ, NC, ks, c, b), jnp.bfloat16)] * j
        + [
            pltpu.VMEM((GRP, ks, c, a), jnp.bfloat16),
            pltpu.VMEM((n, a, ks * a), jnp.bfloat16),
            pltpu.VMEM((2, n, a, b), jnp.float32),
            pltpu.VMEM((GRP, c, b), jnp.bfloat16),
        ]
        + [pltpu.VMEM(half, jnp.bfloat16)] * 4
        + [dma((j + 1,))]
        + [dma((COPIES * j // 2,))] * 2
        + [dma((GRP,))] * 4
        + [dma(half[:2])] * 4,
        compiler_params=pltpu.CompilerParams(collective_id=0, has_side_effects=True, vmem_limit_bytes=48 << 20),
    )(k_irrep, i_irrep, j_irrep, virt_count, amps, turned)
    return out.reshape(i_total, 1, c, b)


def solution(mesh):
    return jax.shard_map(
        shards,
        mesh=mesh,
        in_specs=(P("batch", None, "grp", None), P("batch", "grp", None, None), P(), P(), P(), P()),
        out_specs=P(None, "batch", "grp", None),
        check_vma=False,
    )
```

time: 200 us -> 103 us (0.52)
  waiting for transfers between devices: 108 us -> 0 us
  Pallas kernels: 0 us -> 99.2 us
  blocking collectives: 27.2 us -> 0 us
  starting transfers between devices: 14.9 us -> 0 us
  other arithmetic: 14.8 us -> 0 us
  local copies, waits for them, and re-layouts: 17.7 us -> 3.42 us
  between operations: 13.5 us -> 0.05 us
  matrix products: 3.53 us -> 0 us
    pallas_call x0 -> x1, Pallas kernels: none -> 99.2 us  [shards(): pl.pallas_call(cycle_kernel, out_shape=jax.ShapeDtypeStruct((i_total, c,...]
    all_gather x1 -> x0, waiting for transfers between devices: 48.2 us -> none  [shards(): whole_inter = lax.all_gather(masked_inter, 'grp', axis=1, tiled=True)]
    reduce_scatter x1 -> x0, waiting for transfers between devices: 37.3 us -> none  [shards(): summed = lax.psum_scatter(rounded, 'batch', scatter_dimension=1, tiled=True)]
    all_to_all x1 -> x0, blocking collectives: 27.2 us -> none  [shards(): lax.all_to_all(outgoing, 'grp', split_axis=0, concat_axis=0, tiled=True)]
    all_to_all x1 -> x0, waiting for transfers between devices: 22.7 us -> none  [shards(): lax.all_to_all(masked_amps, 'grp', split_axis=1, concat_axis=2, tiled=True)]
    all_to_all x1 -> x0, starting transfers between devices: 14.8 us -> none  [shards(): lax.all_to_all(masked_amps, 'grp', split_axis=1, concat_axis=2, tiled=True)]
    gather x4 -> x0, local copies, waits for them, and re-layouts: 10.8 us -> none  [the longest x2 7.46 us: shards(): jnp.take_along_axis(inter_blocks, k_source[:, :, None, None, None], axis=1)]
    select_n x5 -> x0, other arithmetic: 8.11 us -> none  [the longest x1 3.45 us: shards(): jnp.take_along_axis(inter_blocks, k_source[:, :, None, None, None], axis=1)]
  transfers between devices with their start and end apart: 3 -> 0, of which waited for: 3 -> 0; matrix products, arithmetic and copies ran while one was open for 4% -> 0% of each run, Pallas kernels for 0% -> 0%
where the time goes in v4:
time: 103 us
  Pallas kernels  99.2 us (96%)
  local copies, waits for them, and re-layouts  3.42 us (3%)
    pallas_call x1, Pallas kernels, shards(): pl.pallas_call(cycle_kernel, out_shape=jax.ShapeDtypeStruct((i_total, c,...  99.2 us
    unnamed x12, local copies, waits for them, and re-layouts  3.42 us

profile of v4, /device:TPU:1, one launch (start us, length us, event | category | flops | bytes accessed | tf_op | source)
XLA Modules:
  0.0 102.7 jit_solution(11081944103237589855)
XLA Ops:
  0.0 0.0 copy-start.4
  0.0 0.9 copy.10
  0.9 0.0 copy-start.1
  0.9 0.0 copy-start.2
  1.0 0.0 copy-start.3
  1.0 0.0 copy-done.4
  1.0 0.6 copy-done.1
  1.6 0.0 copy-done.2
  1.6 0.0 copy-done.3
  1.6 0.0 copy-start
  1.6 1.1 %copy-done = bf16[3,64,16,128]{3,2,1,0:T(8,128)(2,1)S(1)} copy-done((bf16[3,64,16,128]{3,2,1,0:T(8,128)(2,1)S(1)}, bf16[3,64,16,128]{3,2,1,0:T(8,128)(2,1)}, u32[]{:S(2)}) %copy-start) | copy-done | bytes 786456
  2.8 99.2 %shard_map.64 = bf16[64,16,128]{2,1,0:T(8,128)(2,1)S(1)} custom-call(s32[24]{0:T(128)S(1)} %copy-done.1, s32[64]{0:T(128)S(1)} %copy-done.2, s32[8]{0:T(128)S(1)} %copy-done.3, s32[8]{0:T(128)S(1)} %copy-done.4, bf16[3,64,16,128]{3,2,1,0:T(8,128)(2,1)S(1)} %copy-done, bf16[8,3,16,128]{3,2,1,0:T(8,128)(2,1)S(1)} %bitcast.7), custom_call_target="tpu_custom_call" | custom-call | tf_op jit(solution)/shard_map/pallas_call | solution.py:342
  102.0 0.7 copy.12
Async XLA Ops:
  0.0 1.0 copy-start.4
  0.9 0.7 copy-start.1
  0.9 0.7 copy-start.2
  1.0 0.7 copy-start.3
  1.6 1.1 %copy-start = (bf16[3,64,16,128]{3,2,1,0:T(8,128)(2,1)S(1)}, bf16[3,64,16,128]{3,2,1,0:T(8,128)(2,1)}, u32[]{:S(2)}) copy-start(bf16[3,64,16,128]{3,2,1,0:T(8,128)(2,1)} %amps.1) | copy-start | bytes 2359300

commit v5 on v4

--- a/solution.py
+++ b/solution.py
@@ -258,25 +258,25 @@
 
     open_chunk(0)
     lax.fori_loop(1, GRP, start_amps, 0)
-    for t in range(1, far):
-        open_chunk(t)
     for copy in own_blocks:
         copy.wait()
     steps = NZ // 2 + 1
-    for turn in range(1, steps + far):
-        if turn == steps:
-            own_amps.wait()
-            lax.fori_loop(1, GRP, wait_amps, 0)
-            lax.fori_loop(0, n, prepare, 0)
+    lag = 1
+    for turn in range(1, steps + lag * (far - 1) + 2):
         for t in range(far):
-            if 1 <= turn - t <= steps:
-                advance(t, turn - t)
-        t = turn - steps - 1
-        if t >= 0:
-            close_chunk(t)
-            products(t)
-    close_chunk(far - 1)
-    products(far - 1)
+            step = turn - lag * t
+            if step == 0:
+                open_chunk(t)
+            elif 1 <= step <= steps:
+                advance(t, step)
+        for t in range(far):
+            if turn - lag * t == steps + 1:
+                if t == 0:
+                    own_amps.wait()
+                    lax.fori_loop(1, GRP, wait_amps, 0)
+                    lax.fori_loop(0, n, prepare, 0)
+                close_chunk(t)
+                products(t)
 
     def own(r, carry):
         part[0, r] = one(r, high0)

time: 103 us -> 101 us (0.981)
  Pallas kernels: 99.2 us -> 97.2 us
    pallas_call x1, Pallas kernels: 99.2 us -> 97.2 us  [shards(): pl.pallas_call(cycle_kernel, out_shape=jax.ShapeDtypeStruct((i_total, c,...]
where the time goes in v5:
time: 101 us
  Pallas kernels  97.2 us (96%)
  local copies, waits for them, and re-layouts  3.42 us (3%)
    pallas_call x1, Pallas kernels, shards(): pl.pallas_call(cycle_kernel, out_shape=jax.ShapeDtypeStruct((i_total, c,...  97.2 us
    unnamed x12, local copies, waits for them, and re-layouts  3.42 us

profile of v5, /device:TPU:1, one launch (start us, length us, event | category | flops | bytes accessed | tf_op | source)
XLA Modules:
  0.0 100.7 jit_solution(6703840564314797276)
XLA Ops:
  0.0 0.0 copy-start.4
  0.0 0.9 copy.10
  0.9 0.0 copy-start.1
  0.9 0.0 copy-start.2
  1.0 0.0 copy-start.3
  1.0 0.0 copy-done.4
  1.0 0.6 copy-done.1
  1.6 0.0 copy-done.2
  1.6 0.0 copy-done.3
  1.6 0.0 copy-start
  1.6 1.1 %copy-done = bf16[3,64,16,128]{3,2,1,0:T(8,128)(2,1)S(1)} copy-done((bf16[3,64,16,128]{3,2,1,0:T(8,128)(2,1)S(1)}, bf16[3,64,16,128]{3,2,1,0:T(8,128)(2,1)}, u32[]{:S(2)}) %copy-start) | copy-done | bytes 786456
  2.8 97.2 %shard_map.64 = bf16[64,16,128]{2,1,0:T(8,128)(2,1)S(1)} custom-call(s32[24]{0:T(128)S(1)} %copy-done.1, s32[64]{0:T(128)S(1)} %copy-done.2, s32[8]{0:T(128)S(1)} %copy-done.3, s32[8]{0:T(128)S(1)} %copy-done.4, bf16[3,64,16,128]{3,2,1,0:T(8,128)(2,1)S(1)} %copy-done, bf16[8,3,16,128]{3,2,1,0:T(8,128)(2,1)S(1)} %bitcast.7), custom_call_target="tpu_custom_call" | custom-call | tf_op jit(solution)/shard_map/pallas_call | solution.py:342
  100.0 0.7 copy.12
Async XLA Ops:
  0.0 1.0 copy-start.4
  0.9 0.7 copy-start.1
  0.9 0.7 copy-start.2
  1.0 0.7 copy-start.3
  1.6 1.1 %copy-start = (bf16[3,64,16,128]{3,2,1,0:T(8,128)(2,1)S(1)}, bf16[3,64,16,128]{3,2,1,0:T(8,128)(2,1)}, u32[]{:S(2)}) copy-start(bf16[3,64,16,128]{3,2,1,0:T(8,128)(2,1)} %amps.1) | copy-start | bytes 2359300
